TPU v7x, 32 devices: a whole 2x2x4 slice. The times are simulated.
32 devices in a mesh: ctx: 8 (over z, y), head: 4 (over x, core).
Axes of the slice: x: 2, y: 2, z: 4, core: 2. Of those that a mesh axis runs over, the one named last changes fastest.
Arguments:
- query: bfloat16 [2048, 4096], P('ctx', 'head'), may hold values from -6 to 6
- key: bfloat16 [2048, 4096], P('ctx', 'head'), may hold values from -6 to 6
- value: bfloat16 [2048, 4096], P('ctx', 'head'), may hold values from -6 to 6
- episode_lengths: int32 [8], replicated, may hold values from 1 to 1024, 2048 in all
- attn_gain: float32 [4096], P('head'), may hold values from 0.1 to 1.9
- out_weight: bfloat16 [4096, 3072], P('head', 'ctx'), may hold values from -0.09375 to 0.09375
- residual: bfloat16 [2048, 3072], P('ctx', 'head'), may hold values from -36 to 36
- norm_gain: float32 [3072], P('head'), may hold values from 0.1 to 1.9
- expert_ids: int32 [2048, 2], P('ctx'), may hold values from 0 to 7, all different within a row; in each aligned block of 256 rows (0 to 255, 256 to 511, ...) at most 96 rows name the same one
- route_weights: int32 [2048, 2], P('ctx'), may hold values from 4096 to 65535
- gate_weight: bfloat16 [8, 3072, 5120], P('ctx', None, 'head'), may hold values from -0.109375 to 0.109375
- up_weight: bfloat16 [8, 3072, 5120], P('ctx', None, 'head'), may hold values from -0.109375 to 0.109375
- down_weight: bfloat16 [8, 5120, 3072], P('ctx', 'head'), may hold values from -0.125 to 0.125
Outputs:
- layer_out: bfloat16 [2048, 3072], P('ctx', 'head')
Inputs may be any that keep to these rules, and one draw needn't show every extreme that they name: `expert_ids`: in the rows of one device (256 tokens) no expert is named by more than 96 rows, a bound that some block reaches; a row names two different experts.
All inputs are finite; a program needn't handle non-finite values.
Results may differ from a plain program's by a relative error of at most 0.012.
Values may be sent and summed in bfloat16 or wider, within the bound.
A program may use at most 128 MiB of HBM per device.

v0:
```python
import jax
import jax.numpy as jnp
from jax import lax
from jax.sharding import PartitionSpec as P

HEAD_DIM = 128
highest = lax.Precision.HIGHEST


def entering(value, axis, join, neutral):
    place = lax.axis_index(axis)
    gathered = jax.tree.map(
        lambda a, kind: lax.all_gather(a.astype(kind), axis), value, (jnp.bfloat16, jnp.bfloat16)
    )
    state = jax.tree.map(lambda a, e: jnp.zeros_like(a) + jnp.asarray(e, a.dtype), value, neutral)

    def one(step, state):
        return join(
            state,
            jax.tree.map(
                lambda a, own: lax.dynamic_index_in_dim(a, step, 0, False).astype(own.dtype),
                gathered,
                value,
            ),
        )

    return lax.fori_loop(0, place, one, state)


def episode_of(positions, lengths):
    starts = jnp.cumsum(lengths) - lengths
    return jnp.sum((starts[None, :] <= positions[:, None]).astype(jnp.int32), axis=1) - 1


def link_states(earlier, latter):
    marker = jnp.maximum(earlier[0], latter[0])
    joined = jnp.where(latter[0][0] > 0.0, latter[1], earlier[1] + latter[1])
    return (marker, joined)


def on_device(
    query,
    key,
    value,
    episode_lengths,
    attn_gain,
    out_weight,
    residual,
    norm_gain,
    expert_ids,
    route_weights,
    gate_weight,
    up_weight,
    down_weight,
):
    tok_rows = query.shape[0]
    head_size = HEAD_DIM
    heads_local = query.shape[1] // head_size
    own_index = lax.axis_index("ctx")
    ctx_count = lax.axis_size("ctx")
    positions = own_index * tok_rows + jnp.arange(tok_rows, dtype=jnp.int32)
    episode = episode_of(positions, episode_lengths)
    prior = episode_of(positions[:1] - 1, episode_lengths)[0]
    final = episode[-1]
    lifted_query = jax.nn.silu(query.astype(jnp.float32)).reshape(tok_rows, heads_local, head_size)
    lifted_key = jax.nn.silu(key.astype(jnp.float32)).reshape(tok_rows, heads_local, head_size)
    value_rows = value.astype(jnp.float32).reshape(tok_rows, heads_local, head_size)
    keep = (episode == final).astype(jnp.float32)
    state = jnp.einsum(
        "shd,she->hde", lifted_key * keep[:, None, None], value_rows, precision=highest
    )
    marker = (final != prior).astype(jnp.float32).reshape(1)
    blank = (jnp.zeros((1,), jnp.float32), jnp.zeros_like(state))
    carried = entering((marker, state), "ctx", link_states, blank)
    carry_state = carried[1]
    order = jnp.arange(tok_rows, dtype=jnp.int32)
    allowed = ((order[:, None] >= order[None, :]) & (episode[:, None] == episode[None, :])).astype(
        jnp.float32
    )
    scores = jnp.einsum("thd,shd->hts", lifted_query, lifted_key, precision=highest)
    inside = jnp.einsum("hts,shd->thd", scores * allowed[None], value_rows, precision=highest)
    outside = jnp.einsum("thd,hde->the", lifted_query, carry_state, precision=highest)
    attn = inside + outside * (episode == prior).astype(jnp.float32)[:, None, None]
    mean_square = jnp.mean(attn * attn, axis=2, keepdims=True)
    scaled = attn * lax.rsqrt(mean_square + 1e-06) * attn_gain.reshape(heads_local, head_size)
    headed = scaled.reshape(tok_rows, heads_local * head_size).astype(jnp.bfloat16)
    mixed_part = jnp.dot(
        headed,
        lax.all_gather(out_weight, "ctx", axis=1, tiled=True),
        preferred_element_type=jnp.float32,
    )
    width = mixed_part.shape[1]
    mixed_slice = lax.psum_scatter(
        mixed_part.astype(jnp.bfloat16), "head", scatter_dimension=1, tiled=True
    ).astype(jnp.float32)
    hidden_slice = residual.astype(jnp.float32) + mixed_slice
    squares = lax.psum(jnp.sum(hidden_slice * hidden_slice, axis=1), "head")
    normed = (hidden_slice * lax.rsqrt(squares / width + 1e-06)[:, None] * norm_gain).astype(
        jnp.bfloat16
    )
    experts_count = gate_weight.shape[0] * ctx_count
    capacity = 3 * tok_rows // experts_count
    flat_ids = expert_ids.reshape(-1)
    onehot = (flat_ids[:, None] == jnp.arange(experts_count, dtype=jnp.int32)[None, :]).astype(
        jnp.int32
    )
    slot = jnp.sum(jnp.cumsum(onehot, axis=0) * onehot, axis=1) - 1
    source_rows = jnp.repeat(normed, 2, axis=0)
    outgoing = (
        jnp.zeros((experts_count, capacity, normed.shape[1]), jnp.bfloat16)
        .at[flat_ids, slot]
        .set(source_rows)
    )
    raw_weights = route_weights.astype(jnp.float32)
    share = (raw_weights / jnp.sum(raw_weights, axis=1, keepdims=True)).reshape(-1)
    full_rows = lax.all_gather(
        lax.all_to_all(outgoing, "ctx", split_axis=0, concat_axis=0, tiled=True),
        "head",
        axis=2,
        tiled=True,
    )
    flat = full_rows.reshape(-1, full_rows.shape[2])
    gate = jnp.dot(flat, gate_weight[0], preferred_element_type=jnp.float32)
    up = jnp.dot(flat, up_weight[0], preferred_element_type=jnp.float32)
    gated = (jax.nn.silu(gate) * up).astype(jnp.bfloat16)
    partial_value = jnp.dot(gated, down_weight[0], preferred_element_type=jnp.float32).astype(
        jnp.bfloat16
    )
    answer_partial_value = partial_value.reshape(
        full_rows.shape[0], full_rows.shape[1], partial_value.shape[1]
    )
    returned = lax.all_to_all(answer_partial_value, "ctx", split_axis=0, concat_axis=0, tiled=True)
    picked = returned[flat_ids, slot].astype(jnp.float32)
    weighted = jnp.sum((picked * share[:, None]).reshape(tok_rows, 2, picked.shape[1]), axis=1)
    moe = lax.psum_scatter(
        weighted.astype(jnp.bfloat16), "head", scatter_dimension=1, tiled=True
    ).astype(jnp.float32)
    return (hidden_slice + moe).astype(jnp.bfloat16)


def solution(mesh):
    placed = (
        P("ctx", "head"),
        P("ctx", "head"),
        P("ctx", "head"),
        P(),
        P("head"),
        P("head", "ctx"),
        P("ctx", "head"),
        P("head"),
        P("ctx", None),
        P("ctx", None),
        P("ctx", None, "head"),
        P("ctx", None, "head"),
        P("ctx", "head", None),
    )
    return jax.shard_map(
        on_device, mesh=mesh, in_specs=placed, out_specs=P("ctx", "head"), check_vma=False
    )
```

profile of v0, /device:TPU:0, one launch (start us, length us, event | category | flops | bytes accessed | tf_op | source)
XLA Modules:
  0.0 521.8 jit_solution(17571287380999060670)
XLA Ops:
  7.7 0.8 reduce-window.19
  8.6 1.3 fusion.50
  10.5 1.3 convert_multiply_fusion
  12.8 0.6 compare_convert_fusion
  13.4 1.4 convolution_convert_fusion.1
  14.9 0.7 all-gather.5.cloned.1.call-update
  16.2 0.6 dynamic-slice
  16.8 0.7 dynamic-update-slice
  17.5 23.2 %all-reduce = bf16[8]{0:T(256)(128)(2,1)S(1)} all-reduce(bf16[8]{0:T(256)(128)(2,1)S(1)} %dynamic-update-slice), channel_id=1, replica_groups=mesh['ctx'=8,'head'=4] {'ctx'}, use_global_device_ids=true, to_apply=%add | all-reduce | flops 8 | bytes 32
  40.9 3.4 fusion.32
  44.3 22.6 %all-gather.9.cloned.1.call-done = bf16[64,128,128]{2,1,0:T(8,128)(2,1)} async-done(((bf16[8,128,128]{2,1,0:T(8,128)(2,1)}), bf16[64,128,128]{2,1,0:T(8,128)(2,1)}) %all-gather.9.cloned.1.call-update) | async-done | bytes 2097168 | tf_op jit(solution)/shard_map/all_gather | solution.py:13
  67.0 1.3 fusion.23
  68.6 1.5 multiply_reduce_fusion.1
  70.3 96.8 %all-gather.5.cloned.1.call-done = bf16[1024,3072]{1,0:T(8,128)(2,1)} async-done(((bf16[1024,384]{1,0:T(8,128)(2,1)}), bf16[1024,3072]{1,0:T(8,128)(2,1)}) %all-gather.5.cloned.1.call-update) | async-done | bytes 6291472 | tf_op jit(solution)/shard_map/all_gather | solution.py:89
  167.0 5.8 %convolution_convert_fusion = bf16[256,3072]{1,0:T(8,128)(2,1)} fusion(bf16[256,1024]{0,1:T(8,128)(2,1)S(1)} %bitcast.92, bf16[1024,3072]{1,0:T(8,128)(2,1)} %all-gather.5.cloned.1.call-done), kind=kOutput, calls=%fused_computation.13 | convolution fusion | flops 1611399168 | bytes 8388608 | tf_op jit(solution)/shard_map/dot_general | solution.py:87
  173.5 1.1 reduce-window.20
  175.0 24.2 %reduce-scatter.3.cloned.1.call-done = bf16[256,768]{1,0:T(8,128)(2,1)} async-done(((bf16[256,3072]{1,0:T(8,128)(2,1)}), bf16[256,768]{1,0:T(8,128)(2,1)}) %reduce-scatter.3.cloned.1.call-update) | async-done | bytes 393232 | tf_op jit(solution)/shard_map/reduce_scatter | solution.py:93
  199.3 1.2 multiply_reduce_fusion.2
  200.5 5.8 %psum.7 = f32[256]{0:T(256)S(1)} all-reduce(f32[256]{0:T(256)S(1)} %multiply_reduce_fusion.2), channel_id=1, replica_groups=mesh['ctx'=8,'head'=4] {'head'}, use_global_device_ids=true, to_apply=%region_11.12 | all-reduce | flops 256 | bytes 2048 | tf_op jit(solution)/shard_map/psum | solution.py:97
  206.2 1.2 multiply_convert_fusion.1
  208.2 30.3 %scatter_fusion = bf16[8,96,768]{2,1,0:T(8,128)(2,1)S(1)} fusion(bf16[8,96,768]{2,1,0:T(8,128)(2,1)S(1)} %broadcast_in_dim.7, s32[512]{0:T(512)S(1)} %bitcast.88, bf16[512,768]{1,0:T(8,128)(2,1)S(1)} %reshape.237), kind=kCustom, calls=%fused_computation.1 | custom fusion | bytes 2363392 | tf_op jit(solution)/shard_map/scatter | solution.py:112
  238.5 34.4 %all_to_all.10 = bf16[8,96,768]{2,1,0:T(8,128)(2,1)} all-to-all(bf16[8,96,768]{2,1,0:T(8,128)(2,1)S(1)} %scatter_fusion), channel_id=1, replica_groups=mesh['ctx'=8,'head'=4] {'ctx'}, dimensions={0} | all-to-all | bytes 2359296 | tf_op jit(solution)/shard_map/all_to_all | solution.py:117
  272.9 35.3 %all-gather.7.cloned.1.call-done = bf16[8,96,3072]{2,1,0:T(8,128)(2,1)} async-done(((bf16[8,96,768]{2,1,0:T(8,128)(2,1)}), bf16[8,96,3072]{2,1,0:T(8,128)(2,1)}) %all-gather.7.cloned.1.call-update) | async-done | bytes 4718608 | tf_op jit(solution)/shard_map/all_gather | solution.py:116
  308.3 11.7 %fusion.4 = f32[768,1280]{1,0:T(8,128)} fusion(bf16[768,3072]{1,0:T(8,128)(2,1)} %bitcast.98, bf16[1,3072,1280]{2,1,0:T(8,128)(2,1)} %param.25), kind=kOutput, calls=%fused_computation.8 | convolution fusion | flops 6039797760 | bytes 16515072 | tf_op jit(solution)/shard_map/dot_general | solution.py:123
  320.0 22.0 %fusion.6 = bf16[768,3072]{1,0:T(8,128)(2,1)} fusion(bf16[1,1280,3072]{2,1,0:T(8,128)(2,1)} %param.27, bf16[768,3072]{1,0:T(8,128)(2,1)} %bitcast.99, bf16[1,3072,1280]{2,1,0:T(8,128)(2,1)} %param.26, f32[768,1280]{1,0:T(8,128)} %fusion.4), kind=kOutput, calls=%fused_computation.11 | convolution fusion | flops 12087853056 | bytes 29097984 | tf_op jit(solution)/shard_map/dot_general | solution.py:126
  342.0 5.6 %all-to-all-start.1 = ((bf16[8,96,3072]{2,1,0:T(8,128)(2,1)}), bf16[8,96,3072]{2,1,0:T(8,128)(2,1)}, u32[]{:S(2)}, u32[]{:S(2)}) async-start(bf16[8,96,3072]{2,1,0:T(8,128)(2,1)} %bitcast.89), calls=%async_computation.2 | async-start | bytes 9437184 | tf_op jit(solution)/shard_map/all_to_all | solution.py:132
  348.1 104.5 %all-to-all-done.1 = bf16[8,96,3072]{2,1,0:T(8,128)(2,1)} async-done(((bf16[8,96,3072]{2,1,0:T(8,128)(2,1)}), bf16[8,96,3072]{2,1,0:T(8,128)(2,1)}, u32[]{:S(2)}, u32[]{:S(2)}) %all-to-all-start.1) | async-done | bytes 4718624 | tf_op jit(solution)/shard_map/all_to_all | solution.py:132
  452.6 15.1 %gather_fusion = bf16[512,3072]{1,0:T(8,128)(2,1)} fusion(bf16[8,96,3072]{2,1,0:T(8,128)(2,1)} %all-to-all-done.1, s32[512]{0:T(512)S(1)} %bitcast.87), kind=kCustom, calls=%fused_computation | custom fusion | bytes 6295552 | tf_op jit(solution)/shard_map/gather | solution.py:133
  467.7 7.8 %reshape.228 = f32[256,2,3072]{2,1,0:T(2,128)} reshape(bf16[512,3072]{1,0:T(8,128)(2,1)} %gather_fusion) | data formatting | bytes 9437184 | tf_op jit(solution)/shard_map/convert_element_type | solution.py:133
  475.6 11.5 %multiply_reduce_fusion = bf16[256,3072]{1,0:T(8,128)(2,1)} fusion(f32[256,2,3072]{2,1,0:T(2,128)} %reshape.228, f32[256,2]{1,0:T(8,128)S(1)} %copy.50), kind=kLoop, calls=%fused_computation.10 | loop fusion | flops 2359296 | bytes 7866368 | tf_op jit(solution)/shard_map/reduce_sum | solution.py:134
  487.1 26.2 %reduce-scatter.5.cloned.1.call-done = bf16[256,768]{1,0:T(8,128)(2,1)} async-done(((bf16[256,3072]{1,0:T(8,128)(2,1)}), bf16[256,768]{1,0:T(8,128)(2,1)}) %reduce-scatter.5.cloned.1.call-update) | async-done | bytes 393232 | tf_op jit(solution)/shard_map/reduce_scatter | solution.py:135
  513.4 1.9 add_convert_fusion
  (61 shorter events, 4.5 us)
Async XLA Ops:
  6.5 6.9 %copy-start = (bf16[256,1024]{1,0:T(8,128)(2,1)S(1)}, bf16[256,1024]{1,0:T(8,128)(2,1)}, u32[]{:S(2)}) copy-start(bf16[256,1024]{1,0:T(8,128)(2,1)} %param.17) | copy-start | bytes 1572868
  6.5 9.7 %copy-start.10 = (u32[32]{0:T(128)S(1)}, u32[32]{0:T(128)}, u32[]{:S(2)}) copy-start(u32[32]{0:T(128)} %constant.109) | copy-start | bytes 388
  6.5 34.3 %copy-start.9 = (bf16[256,1024]{1,0:T(8,128)(2,1)S(1)}, bf16[256,1024]{1,0:T(8,128)(2,1)}, u32[]{:S(2)}) copy-start(bf16[256,1024]{1,0:T(8,128)(2,1)} %param.15) | copy-start | bytes 1572868
  6.5 60.4 %all-gather.9.cloned.1.call-start = ((), (), s32[]{:S(2)}) async-start(), calls=%async_computation.8 | async-start | bytes 2359296 | tf_op jit(solution)/shard_map/all_gather | solution.py:13
  14.8 152.2 %all-gather.5.cloned.1.call-start = ((), (), s32[]{:S(2)}) async-start(), calls=%async_computation.4 | async-start | bytes 7077888 | tf_op jit(solution)/shard_map/all_gather | solution.py:89
  15.6 183.7 %reduce-scatter.3.cloned.1.call-start = ((), (), s32[]{:S(2)}) async-start(), calls=%async_computation.5 | async-start | bytes 1966080 | tf_op jit(solution)/shard_map/reduce_scatter | solution.py:93
  67.0 1.6 copy-start.4
  67.0 3.1 copy-start.6
  167.0 5.9 %copy-start.8 = (s32[256,2]{0,1:T(2,128)S(1)}, s32[256,2]{0,1:T(2,128)}, u32[]{:S(2)}) copy-start(s32[256,2]{0,1:T(2,128)} %param.23) | copy-start | bytes 6148
  167.0 32.2 %copy-start.2 = (bf16[256,768]{1,0:T(8,128)(2,1)S(1)}, bf16[256,768]{1,0:T(8,128)(2,1)}, u32[]{:S(2)}) copy-start(bf16[256,768]{1,0:T(8,128)(2,1)} %param.21) | copy-start | bytes 1179652
  167.0 39.2 %copy-start.7 = (f32[768]{0:T(1024)S(1)}, f32[768]{0:T(1024)}, u32[]{:S(2)}) copy-start(f32[768]{0:T(1024)} %param.22) | copy-start | bytes 9220
  172.9 135.4 %all-gather.7.cloned.1.call-start = ((), (), s32[]{:S(2)}) async-start(), calls=%async_computation.6 | async-start | bytes 5898240 | tf_op jit(solution)/shard_map/all_gather | solution.py:116
  342.0 5.9 %copy-start.5 = (s32[256,2]{0,1:T(2,128)S(1)}, s32[256,2]{0,1:T(2,128)}, u32[]{:S(2)}) copy-start(s32[256,2]{0,1:T(2,128)} %param.24) | copy-start | bytes 6148
  342.0 110.6 %all-to-all-start.1 = ((bf16[8,96,3072]{2,1,0:T(8,128)(2,1)}), bf16[8,96,3072]{2,1,0:T(8,128)(2,1)}, u32[]{:S(2)}, u32[]{:S(2)}) async-start(bf16[8,96,3072]{2,1,0:T(8,128)(2,1)} %bitcast.89), calls=%async_computation.2 | async-start | bytes 9437184 | tf_op jit(solution)/shard_map/all_to_all | solution.py:132
  347.7 165.7 %reduce-scatter.5.cloned.1.call-start = ((), (), s32[]{:S(2)}) async-start(), calls=%async_computation.7 | async-start | bytes 1966080 | tf_op jit(solution)/shard_map/reduce_scatter | solution.py:135
  467.7 47.5 %copy-start.1 = (bf16[256,1024]{1,0:T(8,128)(2,1)S(1)}, bf16[256,1024]{1,0:T(8,128)(2,1)}, u32[]{:S(2)}) copy-start(bf16[256,1024]{1,0:T(8,128)(2,1)} %param.17) | copy-start | bytes 1572868
  475.6 37.8 %copy-start.3 = (bf16[256,768]{1,0:T(8,128)(2,1)S(1)}, bf16[256,768]{1,0:T(8,128)(2,1)}, u32[]{:S(2)}) copy-start(bf16[256,768]{1,0:T(8,128)(2,1)} %reduce-scatter.3.cloned.1.call-done) | copy-start | bytes 1179652
Sparse Core Ops, SparseCore 0:
  14.9 51.9 all-gather.8
  69.0 98.0 all-gather.4
  173.0 26.2 reduce-scatter.2
  273.0 35.1 all-gather.6
  487.3 26.0 reduce-scatter.4
where the time goes:
time: 523 us; the launch traced here: 522 us
  waiting for transfers between devices  310 us (59%)
  blocking collectives  63.4 us (12%)
  local copies, waits for them, and re-layouts  58 us (11%)
  matrix products  47.1 us (9%)
  other arithmetic  21.5 us (4%)
  between operations  15.3 us (3%)
  starting transfers between devices  6.03 us (1%)
    all_to_all x1, waiting for transfers between devices, on_device(): lax.all_to_all(answer_partial_value, 'ctx', split_axis=0, concat_axis=0,...  104 us
    all_gather x1, waiting for transfers between devices, on_device(): lax.all_gather(out_weight, 'ctx', axis=1, tiled=True)  96.8 us
    all_gather x1, waiting for transfers between devices, on_device(): lax.all_gather(lax.all_to_all(outgoing, 'ctx', split_axis=0, concat_axis=...  35.3 us
    all_to_all x1, blocking collectives, on_device(): lax.all_to_all(outgoing, 'ctx', split_axis=0, concat_axis=0, tiled=True)  34.4 us
    scatter x1, local copies, waits for them, and re-layouts, on_device(): outgoing = jnp.zeros((experts_count, capacity, normed.shape[1]), jnp.bflo...  30.3 us
    reduce_scatter x1, waiting for transfers between devices, on_device(): lax.psum_scatter(weighted.astype(jnp.bfloat16), 'head', scatter_dimension...  26.2 us
    reduce_scatter x1, waiting for transfers between devices, on_device(): lax.psum_scatter(mixed_part.astype(jnp.bfloat16), 'head', scatter_dimensi...  24.2 us
    unnamed x1, blocking collectives  23.2 us
  transfers between devices with their start and end apart: 6, of which 6 were waited for; matrix products, arithmetic and copies ran while one was open for 2% of the time, Pallas kernels for 0%

commit v1 on v0

--- a/solution.py
+++ b/solution.py
@@ -5,6 +5,17 @@
 
 HEAD_DIM = 128
 highest = lax.Precision.HIGHEST
+
+
+def gather_around(x, axis, dim):
+    ways = lax.axis_size(axis)
+    pieces = [x]
+    for far in range(1, ways):
+        pieces.append(
+            lax.ppermute(pieces[far - 1], axis, [(d, (d - 1) % ways) for d in range(ways)])
+        )
+    line = jnp.concatenate(pieces, axis=dim)
+    return jnp.roll(line, lax.axis_index(axis) * x.shape[dim], axis=dim)
 
 
 def entering(value, axis, join, neutral):
@@ -113,11 +124,8 @@
     )
     raw_weights = route_weights.astype(jnp.float32)
     share = (raw_weights / jnp.sum(raw_weights, axis=1, keepdims=True)).reshape(-1)
-    full_rows = lax.all_gather(
-        lax.all_to_all(outgoing, "ctx", split_axis=0, concat_axis=0, tiled=True),
-        "head",
-        axis=2,
-        tiled=True,
+    full_rows = gather_around(
+        lax.all_to_all(outgoing, "ctx", split_axis=0, concat_axis=0, tiled=True), "head", 2
     )
     flat = full_rows.reshape(-1, full_rows.shape[2])
     gate = jnp.dot(flat, gate_weight[0], preferred_element_type=jnp.float32)

time: 523 us -> 559 us (1.069)
  local copies, waits for them, and re-layouts: 58 us -> 86.5 us
    ppermute x0 -> x3, waiting for transfers between devices: none -> 39.7 us  [gather_around(): lax.ppermute(pieces[far - 1], axis, [(d, (d - 1) % ways) for d in range(w...]
    all_gather x1 -> x0, waiting for transfers between devices: 35.3 us -> none  [on_device(): lax.all_gather(lax.all_to_all(outgoing, 'ctx', split_axis=0, concat_axis=...]
    scatter x1, local copies, waits for them, and re-layouts: 30.3 us -> 46.9 us  [on_device(): outgoing = jnp.zeros((experts_count, capacity, normed.shape[1]), jnp.bflo...]
    unnamed x26 -> x37, local copies, waits for them, and re-layouts: 1.8 us -> 8.71 us
  transfers between devices with their start and end apart: 6 -> 8, of which waited for: 6 -> 8; matrix products, arithmetic and copies ran while one was open for 2% -> 3% of each run, Pallas kernels for 0% -> 0%
where the time goes in v1:
time: 559 us; the launch traced here: 555 us
  waiting for transfers between devices  314 us (56%)
  local copies, waits for them, and re-layouts  86.5 us (15%)
  blocking collectives  63.1 us (11%)
  matrix products  45.7 us (8%)
  other arithmetic  21.6 us (4%)
  between operations  15.3 us (3%)
  starting transfers between devices  8.79 us (2%)
    all_to_all x1, waiting for transfers between devices, on_device(): lax.all_to_all(answer_partial_value, 'ctx', split_axis=0, concat_axis=0,...  106 us
    all_gather x1, waiting for transfers between devices, on_device(): lax.all_gather(out_weight, 'ctx', axis=1, tiled=True)  95.9 us
    scatter x1, local copies, waits for them, and re-layouts, on_device(): outgoing = jnp.zeros((experts_count, capacity, normed.shape[1]), jnp.bflo...  46.9 us
    ppermute x3, waiting for transfers between devices, gather_around(): lax.ppermute(pieces[far - 1], axis, [(d, (d - 1) % ways) for d in range(w...  39.7 us
    all_to_all x1, blocking collectives, on_device(): lax.all_to_all(outgoing, 'ctx', split_axis=0, concat_axis=0, tiled=True)  34.1 us
    reduce_scatter x1, waiting for transfers between devices, on_device(): lax.psum_scatter(weighted.astype(jnp.bfloat16), 'head', scatter_dimension...  26.1 us
    reduce_scatter x1, waiting for transfers between devices, on_device(): lax.psum_scatter(mixed_part.astype(jnp.bfloat16), 'head', scatter_dimensi...  24.3 us
    unnamed x1, blocking collectives  23.2 us
  transfers between devices with their start and end apart: 8, of which 8 were waited for; matrix products, arithmetic and copies ran while one was open for 3% of the time, Pallas kernels for 0%

profile of v1, /device:TPU:0, one launch (start us, length us, event | category | flops | bytes accessed | tf_op | source)
XLA Modules:
  0.0 555.2 jit_solution(4291294224453770735)
XLA Ops:
  13.4 1.4 convolution_convert_fusion.1
  17.5 23.2 %all-reduce = bf16[8]{0:T(256)(128)(2,1)S(1)} all-reduce(bf16[8]{0:T(256)(128)(2,1)S(1)} %dynamic-update-slice), channel_id=1, replica_groups=mesh['ctx'=8,'head'=4] {'ctx'}, use_global_device_ids=true, to_apply=%add | all-reduce | flops 8 | bytes 32
  40.9 4.5 fusion.31
  45.3 21.6 %all-gather.6.cloned.1.call-done = bf16[64,128,128]{2,1,0:T(8,128)(2,1)} async-done(((bf16[8,128,128]{2,1,0:T(8,128)(2,1)}), bf16[64,128,128]{2,1,0:T(8,128)(2,1)}) %all-gather.6.cloned.1.call-update) | async-done | bytes 2097168 | tf_op jit(solution)/shard_map/all_gather | solution.py:24
  67.0 2.5 fusion.22
  69.5 1.4 multiply_reduce_fusion.1
  71.1 95.9 %all-gather.4.cloned.1.call-done = bf16[1024,3072]{1,0:T(8,128)(2,1)} async-done(((bf16[1024,384]{1,0:T(8,128)(2,1)}), bf16[1024,3072]{1,0:T(8,128)(2,1)}) %all-gather.4.cloned.1.call-update) | async-done | bytes 6291472 | tf_op jit(solution)/shard_map/all_gather | solution.py:100
  167.0 5.8 %convolution_convert_fusion = bf16[256,3072]{1,0:T(8,128)(2,1)} fusion(bf16[256,1024]{0,1:T(8,128)(2,1)S(1)} %bitcast.92, bf16[1024,3072]{1,0:T(8,128)(2,1)} %all-gather.4.cloned.1.call-done), kind=kOutput, calls=%fused_computation.13 | convolution fusion | flops 1611399168 | bytes 8388608 | tf_op jit(solution)/shard_map/dot_general | solution.py:98
  175.0 24.3 %reduce-scatter.3.cloned.1.call-done = bf16[256,768]{1,0:T(8,128)(2,1)} async-done(((bf16[256,3072]{1,0:T(8,128)(2,1)}), bf16[256,768]{1,0:T(8,128)(2,1)}) %reduce-scatter.3.cloned.1.call-update) | async-done | bytes 393232 | tf_op jit(solution)/shard_map/reduce_scatter | solution.py:104
  200.4 5.8 %psum.7 = f32[256]{0:T(256)S(1)} all-reduce(f32[256]{0:T(256)S(1)} %multiply_reduce_fusion.2), channel_id=1, replica_groups=mesh['ctx'=8,'head'=4] {'head'}, use_global_device_ids=true, to_apply=%region_11.12 | all-reduce | flops 256 | bytes 2048 | tf_op jit(solution)/shard_map/psum | solution.py:108
  209.0 46.9 %scatter_fusion = bf16[8,96,768]{2,1,0:T(8,128)(2,1)S(1)} fusion(bf16[8,96,768]{2,1,0:T(8,128)(2,1)S(1)} %broadcast_in_dim.7, s32[512]{0:T(512)S(1)} %bitcast.86, bf16[512,768]{1,0:T(8,128)(2,1)} %reshape.237), kind=kCustom, calls=%fused_computation.1 | custom fusion | bytes 2363392 | tf_op jit(solution)/shard_map/scatter | solution.py:123
  256.0 34.1 %all_to_all.10 = bf16[8,96,768]{2,1,0:T(8,128)(2,1)S(1)} all-to-all(bf16[8,96,768]{2,1,0:T(8,128)(2,1)S(1)} %scatter_fusion), channel_id=1, replica_groups=mesh['ctx'=8,'head'=4] {'ctx'}, dimensions={0} | all-to-all | bytes 2359296 | tf_op jit(solution)/shard_map/all_to_all | solution.py:128
  290.1 13.7 %collective-permute-done = bf16[8,96,768]{2,1,0:T(8,128)(2,1)S(1)} collective-permute-done((bf16[8,96,768]{2,1,0:T(8,128)(2,1)S(1)}, bf16[8,96,768]{2,1,0:T(8,128)(2,1)S(1)}, u32[]{:S(2)}, u32[]{:S(2)}) %collective-permute-start) | collective-permute-done | bytes 1179680 | tf_op jit(solution)/shard_map/ppermute | solution.py:15
  303.8 1.9 collective-permute-start.1
  305.7 13.7 %collective-permute-done.1 = bf16[8,96,768]{2,1,0:T(8,128)(2,1)} collective-permute-done((bf16[8,96,768]{2,1,0:T(8,128)(2,1)S(1)}, bf16[8,96,768]{2,1,0:T(8,128)(2,1)}, u32[]{:S(2)}, u32[]{:S(2)}) %collective-permute-start.1) | collective-permute-done | bytes 1179680 | tf_op jit(solution)/shard_map/ppermute | solution.py:15
  319.5 2.0 collective-permute-start.2
  321.8 1.4 constant_dynamic-update-slice_fusion.5
  323.2 12.3 %collective-permute-done.2 = bf16[8,96,768]{2,1,0:T(8,128)(2,1)} collective-permute-done((bf16[8,96,768]{2,1,0:T(8,128)(2,1)}, bf16[8,96,768]{2,1,0:T(8,128)(2,1)}, u32[]{:S(2)}, u32[]{:S(2)}) %collective-permute-start.2) | collective-permute-done | bytes 1179680 | tf_op jit(solution)/shard_map/ppermute | solution.py:15
  335.5 1.4 constant_dynamic-update-slice_fusion.4
  337.3 1.6 constant_dynamic-update-slice_fusion.1
  338.8 1.5 constant_dynamic-update-slice_fusion
  340.3 2.6 constant_dynamic-slice_fusion.1
  342.9 2.2 copy-done.2
  345.1 8.2 %fusion.4 = f32[768,1280]{1,0:T(8,128)} fusion(bf16[768,3072]{1,0:T(8,128)(2,1)S(1)} %bitcast.88, bf16[1,3072,1280]{2,1,0:T(8,128)(2,1)S(1)} %bitcast.99), kind=kOutput, calls=%fused_computation.8 | convolution fusion | flops 6039797760 | bytes 16515072 | tf_op jit(solution)/shard_map/dot_general | solution.py:131
  353.3 22.0 %fusion.6 = bf16[768,3072]{1,0:T(8,128)(2,1)} fusion(bf16[1,1280,3072]{2,1,0:T(8,128)(2,1)} %param.27, f32[768,1280]{1,0:T(8,128)} %fusion.4, bf16[768,3072]{1,0:T(8,128)(2,1)} %bitcast.89, bf16[1,3072,1280]{2,1,0:T(8,128)(2,1)} %param.26), kind=kOutput, calls=%fused_computation.11 | convolution fusion | flops 12087853056 | bytes 29097984 | tf_op jit(solution)/shard_map/dot_general | solution.py:134
  375.2 4.7 all-to-all-start.1
  380.2 105.9 %all-to-all-done.1 = bf16[8,96,3072]{2,1,0:T(8,128)(2,1)} async-done(((bf16[8,96,3072]{2,1,0:T(8,128)(2,1)}), bf16[8,96,3072]{2,1,0:T(8,128)(2,1)}, u32[]{:S(2)}, u32[]{:S(2)}) %all-to-all-start.1) | async-done | bytes 4718624 | tf_op jit(solution)/shard_map/all_to_all | solution.py:140
  486.1 15.1 %gather_fusion = bf16[512,3072]{1,0:T(8,128)(2,1)} fusion(bf16[8,96,3072]{2,1,0:T(8,128)(2,1)} %all-to-all-done.1, s32[512]{0:T(512)S(1)} %bitcast.85), kind=kCustom, calls=%fused_computation | custom fusion | bytes 6295552 | tf_op jit(solution)/shard_map/gather | solution.py:141
  501.3 7.8 %reshape.228 = f32[256,2,3072]{2,1,0:T(2,128)} reshape(bf16[512,3072]{1,0:T(8,128)(2,1)} %gather_fusion) | data formatting | bytes 9437184 | tf_op jit(solution)/shard_map/convert_element_type | solution.py:141
  509.1 11.5 %multiply_reduce_fusion = bf16[256,3072]{1,0:T(8,128)(2,1)} fusion(f32[256,2,3072]{2,1,0:T(2,128)} %reshape.228, f32[256,2]{1,0:T(8,128)S(1)} %copy.50), kind=kLoop, calls=%fused_computation.10 | loop fusion | flops 2359296 | bytes 7866368 | tf_op jit(solution)/shard_map/reduce_sum | solution.py:142
  520.7 26.1 %reduce-scatter.5.cloned.1.call-done = bf16[256,768]{1,0:T(8,128)(2,1)} async-done(((bf16[256,3072]{1,0:T(8,128)(2,1)}), bf16[256,768]{1,0:T(8,128)(2,1)}) %reduce-scatter.5.cloned.1.call-update) | async-done | bytes 393232 | tf_op jit(solution)/shard_map/reduce_scatter | solution.py:143
  546.8 1.9 add_convert_fusion
  (78 shorter events, 15.0 us)
Async XLA Ops:
  6.5 6.8 %copy-start = (bf16[256,1024]{1,0:T(8,128)(2,1)S(1)}, bf16[256,1024]{1,0:T(8,128)(2,1)}, u32[]{:S(2)}) copy-start(bf16[256,1024]{1,0:T(8,128)(2,1)} %param.17) | copy-start | bytes 1572868
  6.5 9.6 %copy-start.10 = (u32[32]{0:T(128)S(1)}, u32[32]{0:T(128)}, u32[]{:S(2)}) copy-start(u32[32]{0:T(128)} %constant.132) | copy-start | bytes 388
  6.5 60.4 %all-gather.6.cloned.1.call-start = ((), (), s32[]{:S(2)}) async-start(), calls=%async_computation.7 | async-start | bytes 2359296 | tf_op jit(solution)/shard_map/all_gather | solution.py:24
  14.8 152.2 %all-gather.4.cloned.1.call-start = ((), (), s32[]{:S(2)}) async-start(), calls=%async_computation.4 | async-start | bytes 7077888 | tf_op jit(solution)/shard_map/all_gather | solution.py:100
  15.5 183.7 %reduce-scatter.3.cloned.1.call-start = ((), (), s32[]{:S(2)}) async-start(), calls=%async_computation.5 | async-start | bytes 1966080 | tf_op jit(solution)/shard_map/reduce_scatter | solution.py:104
  66.9 2.5 copy-start.5
  67.0 4.0 copy-start.7
  167.0 5.8 %copy-start.9 = (s32[256,2]{0,1:T(2,128)S(1)}, s32[256,2]{0,1:T(2,128)}, u32[]{:S(2)}) copy-start(s32[256,2]{0,1:T(2,128)} %param.23) | copy-start | bytes 6148
  167.0 32.2 %copy-start.3 = (bf16[256,768]{1,0:T(8,128)(2,1)S(1)}, bf16[256,768]{1,0:T(8,128)(2,1)}, u32[]{:S(2)}) copy-start(bf16[256,768]{1,0:T(8,128)(2,1)} %param.21) | copy-start | bytes 1179652
  167.0 39.2 %copy-start.8 = (f32[768]{0:T(1024)S(1)}, f32[768]{0:T(1024)}, u32[]{:S(2)}) copy-start(f32[768]{0:T(1024)} %param.22) | copy-start | bytes 9220
  290.1 13.7 %collective-permute-start = (bf16[8,96,768]{2,1,0:T(8,128)(2,1)S(1)}, bf16[8,96,768]{2,1,0:T(8,128)(2,1)S(1)}, u32[]{:S(2)}, u32[]{:S(2)}) collective-permute-start(bf16[8,96,768]{2,1,0:T(8,128)(2,1)S(1)} %all_to_all.10), channel_id=1, source_target_pairs={{0,3},{1,0},{2,1},{3,2},{4,7},{5,4},{6,5},{7,6},{8,11},{9,8},{10,9... | collective-permute-start | bytes 3538952 | tf_op jit(solution)/shard_map/ppermute | solution.py:15
  303.8 15.6 %collective-permute-start.1 = (bf16[8,96,768]{2,1,0:T(8,128)(2,1)S(1)}, bf16[8,96,768]{2,1,0:T(8,128)(2,1)}, u32[]{:S(2)}, u32[]{:S(2)}) collective-permute-start(bf16[8,96,768]{2,1,0:T(8,128)(2,1)S(1)} %collective-permute-done), channel_id=1, source_target_pairs={{0,3},{1,0},{2,1},{3,2},{4,7},{5,4},{6,5},{7,6},{8,11},{9,8},{10,9... | collective-permute-start | bytes 3538952 | tf_op jit(solution)/shard_map/ppermute | solution.py:15
  319.5 16.0 %collective-permute-start.2 = (bf16[8,96,768]{2,1,0:T(8,128)(2,1)}, bf16[8,96,768]{2,1,0:T(8,128)(2,1)}, u32[]{:S(2)}, u32[]{:S(2)}) collective-permute-start(bf16[8,96,768]{2,1,0:T(8,128)(2,1)} %collective-permute-done.1), channel_id=1, source_target_pairs={{0,3},{1,0},{2,1},{3,2},{4,7},{5,4},{6,5},{7,6},{8,11},{9,8},{10,9... | collective-permute-start | bytes 3538952 | tf_op jit(solution)/shard_map/ppermute | solution.py:15
  337.3 7.8 %slice-start = ((s8[7864320]{0:T(1024)(128)(4,1)}), s8[4194304]{0:T(1024)(128)(4,1)S(1)}, s32[]{:S(2)}) async-start(s8[7864320]{0:T(1024)(128)(4,1)} %bitcast.98), calls=%async_computation.8 | async-start | bytes 8388608
  340.3 4.7 slice-start.1
  342.9 2.2 copy-start.2
  375.2 4.8 copy-start.6
  375.2 110.9 %all-to-all-start.1 = ((bf16[8,96,3072]{2,1,0:T(8,128)(2,1)}), bf16[8,96,3072]{2,1,0:T(8,128)(2,1)}, u32[]{:S(2)}, u32[]{:S(2)}) async-start(bf16[8,96,3072]{2,1,0:T(8,128)(2,1)} %bitcast.87), calls=%async_computation.2 | async-start | bytes 9437184 | tf_op jit(solution)/shard_map/all_to_all | solution.py:140
  380.0 166.8 %reduce-scatter.5.cloned.1.call-start = ((), (), s32[]{:S(2)}) async-start(), calls=%async_computation.6 | async-start | bytes 1966080 | tf_op jit(solution)/shard_map/reduce_scatter | solution.py:143
  501.3 47.4 %copy-start.1 = (bf16[256,1024]{1,0:T(8,128)(2,1)S(1)}, bf16[256,1024]{1,0:T(8,128)(2,1)}, u32[]{:S(2)}) copy-start(bf16[256,1024]{1,0:T(8,128)(2,1)} %param.17) | copy-start | bytes 1572868
  509.1 37.7 %copy-start.4 = (bf16[256,768]{1,0:T(8,128)(2,1)S(1)}, bf16[256,768]{1,0:T(8,128)(2,1)}, u32[]{:S(2)}) copy-start(bf16[256,768]{1,0:T(8,128)(2,1)} %reduce-scatter.3.cloned.1.call-done) | copy-start | bytes 1179652
Sparse Core Ops, SparseCore 0:
  14.9 51.9 all-gather.5
  69.0 98.0 all-gather.3
  173.0 26.2 reduce-scatter.2
  520.8 25.9 reduce-scatter.4
